TPU v7x, 128 devices: a whole 4x4x4 slice. The times are simulated.
128 devices in a mesh: space: 16 (over y, x_lo, core), filt: 8 (over x_hi, z).
Axes of the slice: x: 4 (x_hi: 2, x_lo: 2; x = x_hi * 2 + x_lo), y: 4, z: 4, core: 2. Of those that a mesh axis runs over, the one named last changes fastest.
Arguments:
- volume: bfloat16 [64, 128, 16, 128], P('space', 'filt'), may hold values from -6 to 6
- w_early: bfloat16 [27, 128, 128], replicated, may hold values from -0.109375 to 0.109375
- w_deep: bfloat16 [27, 128, 256], P(None, None, 'filt'), may hold values from -0.109375 to 0.109375
- cotangent: bfloat16 [32, 64, 8, 256], P('space', None, None, 'filt'), may hold values from -6 to 6
Outputs:
- block_out: bfloat16 [32, 64, 8, 256], P('space', None, None, 'filt')
- grad_early: float32 [27, 128, 128], replicated
- grad_deep: float32 [27, 128, 256], P(None, None, 'filt')
All inputs are finite; a program needn't handle non-finite values.
Results may differ from a plain program's by a relative error of at most 0.0059.
Values may be sent and summed in bfloat16 or wider, within the bound.
A program may use at most 128 MiB of HBM per device.

v0:
```python
import math
import jax
import jax.numpy as jnp
from jax import lax
from jax.sharding import PartitionSpec as P


def extended(block, sides, width):
    for axis, dim in sides:
        count = lax.axis_size(axis)
        forward = [(i, i + 1) for i in range(count - 1)]
        backward = [(target, source) for source, target in forward]
        low = lax.ppermute(
            lax.slice_in_dim(block, block.shape[dim] - width, None, axis=dim), axis, forward
        )
        high = lax.ppermute(lax.slice_in_dim(block, 0, width, axis=dim), axis, backward)
        block = jnp.concatenate([low, block, high], axis=dim)
    return block


def silu_grad(value):
    sig = jax.nn.sigmoid(value)
    return sig * (1.0 + value * (1.0 - sig))


def window(source, tap, size_x, size_y, size_z):
    first = tap // 9
    second = tap // 3 % 3
    third = tap % 3
    part = source[first : first + size_x, second : second + size_y, third : third + size_z]
    return part.reshape(size_x * size_y * size_z, source.shape[3])


def contract_cells(left, right):
    return lax.dot_general(
        left, right, (((0,), (0,)), ((), ())), preferred_element_type=jnp.float32
    )


def shards(volume, w_early, w_deep, cotangent):
    size_x, size_y, size_z, cin = volume.shape
    width = w_early.shape[2]
    cells = size_x * size_y * size_z
    rimmed = extended(volume, (("space", 0), ("filt", 1)), 1)
    padded = jnp.pad(rimmed, ((0, 0), (0, 0), (1, 1), (0, 0)))
    pre_early = jnp.zeros((cells, width), jnp.float32)
    for tap in range(27):
        pre_early = pre_early + jnp.dot(
            window(padded, tap, size_x, size_y, size_z),
            w_early[tap],
            preferred_element_type=jnp.float32,
        )
    pooled = (
        jax.nn.silu(pre_early)
        .reshape(size_x // 2, 2, size_y // 2, 2, size_z // 2, 2, width)
        .mean(axis=(1, 3, 5))
        .astype(jnp.bfloat16)
    )
    local = lax.all_to_all(pooled, "filt", split_axis=3, concat_axis=1, tiled=True)
    half_x, full_y, half_z, shard_c = local.shape
    deep_cells = half_x * full_y * half_z
    filters = w_deep.shape[2]
    slab = extended(local, (("space", 0),), 1)
    slab = jnp.pad(slab, ((0, 0), (1, 1), (1, 1), (0, 0)))

    def kernel_terms(piece):
        return jnp.stack(
            [
                contract_cells(window(piece, tap, half_x, full_y, half_z), grad_pre_deep)
                for tap in range(27)
            ]
        )

    empty = jnp.zeros((deep_cells, filters), jnp.float32)
    total = empty
    piece = lax.all_gather(slab, "filt", axis=3, tiled=True)
    for forward_tap in range(27):
        rows = w_deep[forward_tap]
        total = total + jnp.dot(
            window(piece, forward_tap, half_x, full_y, half_z),
            rows,
            preferred_element_type=jnp.float32,
        )
    block_out = jax.nn.silu(total).astype(jnp.bfloat16).reshape(half_x, full_y, half_z, filters)
    grad_pre_deep = (
        cotangent.reshape(deep_cells, filters).astype(jnp.float32) * silu_grad(total)
    ).astype(jnp.bfloat16)
    deep_terms = kernel_terms(lax.all_gather(slab, "filt", axis=3, tiled=True))
    deep_total = deep_cells * lax.axis_size("space")
    grad_deep = lax.psum(deep_terms, "space") / math.sqrt(deep_total)
    grid_grad = grad_pre_deep.reshape(half_x, full_y, half_z, filters)
    grad_slab = extended(grid_grad, (("space", 0),), 1)
    grad_slab = jnp.pad(grad_slab, ((0, 0), (1, 1), (1, 1), (0, 0)))
    term = jnp.zeros((deep_cells, width), jnp.float32)
    for tap in range(27):
        term = term + jnp.dot(
            window(grad_slab, 26 - tap, half_x, full_y, half_z),
            w_deep[tap].T,
            preferred_element_type=jnp.float32,
        )
    term = term.reshape(half_x, full_y, half_z, width)
    mine = lax.psum_scatter(term, "filt", scatter_dimension=3, tiled=True).astype(jnp.bfloat16)
    grad_pooled = lax.all_to_all(mine, "filt", split_axis=1, concat_axis=3, tiled=True)
    spread = jnp.broadcast_to(
        grad_pooled.astype(jnp.float32)[:, None, :, None, :, None, :],
        (size_x // 2, 2, size_y // 2, 2, size_z // 2, 2, width),
    )
    spread = spread.reshape(cells, width) / 8.0
    grad_pre_early = (spread * silu_grad(pre_early)).astype(jnp.bfloat16)
    early_terms = jnp.stack(
        [
            contract_cells(window(padded, tap, size_x, size_y, size_z), grad_pre_early)
            for tap in range(27)
        ]
    )
    early_total = cells * lax.axis_size("space") * lax.axis_size("filt")
    grad_early = lax.psum(early_terms, ("space", "filt")) / math.sqrt(early_total)
    return (block_out, grad_early, grad_deep)


def solution(mesh):
    return jax.shard_map(
        shards,
        mesh=mesh,
        in_specs=(
            P("space", "filt", None, None),
            P(),
            P(None, None, "filt"),
            P("space", None, None, "filt"),
        ),
        out_specs=(P("space", None, None, "filt"), P(), P(None, None, "filt")),
        check_vma=False,
    )
```

profile of v0, /device:TPU:1, one launch (start us, length us, event | category | flops | bytes accessed | tf_op | source)
XLA Modules:
  0.0 586.7 jit_solution(7086958504121832827)
XLA Ops:
  8.9 4.5 collective-permute-start
  15.4 3.6 collective-permute-done.1
  20.4 3.5 collective-permute-start.2
  25.3 3.4 collective-permute-done.3
  38.9 14.4 %all_to_all.27 = bf16[8,2,1024]{2,1,0:T(2,128)(2,1)S(1)} all-to-all(bf16[8,2,1024]{2,1,0:T(2,128)(2,1)S(1)} %reshape.420), channel_id=1, replica_groups=mesh['space'=16,'filt'=8] {'filt'}, dimensions={0} | all-to-all | bytes 65536 | tf_op jit(solution)/shard_map/all_to_all | solution.py:59
  54.5 2.3 collective-permute-start.5
  56.8 3.7 collective-permute-start.4
  63.2 32.5 %all_gather.4 = bf16[4,66,10,128]{1,0,2,3:T(4,128)(2,1)S(1)} all-gather(bf16[4,66,10,16]{1,0,2,3:T(4,128)(2,1)S(1)} %pad.13.clone), channel_id=1, replica_groups=mesh['space'=16,'filt'=8] {'filt'}, dimensions={3}, use_global_device_ids=true | all-gather | bytes 760320 | tf_op jit(solution)/shard_map/all_gather | solution.py:76
  95.7 5.0 fusion.249
  100.7 12.2 %fusion.248 = (bf16[2,64,8,128]{1,0,2,3:T(2,128)(2,1)}, bf16[2,64,8,128]{1,0,2,3:T(2,128)(2,1)S(1)}, bf16[2,64,8,128]{1,0,2,3:T(2,128)(2,1)}, bf16[2,64,8,128]{1...) fusion(bf16[4,66,10,128]{1,0,2,3:T(4,128)(2,1)S(1)} %all_gather.4), kind=kLoop, calls=%fused_computation.410 | loop fusion | bytes 9961472 | tf_op jit(solution)/shard_map/slice | solution.py:30
  114.5 2.2 copy.199
  118.9 2.2 copy.197
  121.2 2.3 copy.196
  123.4 2.2 copy.195
  125.7 2.2 copy.194
  127.9 2.2 copy.193
  130.2 2.2 copy.219
  142.5 2.2 copy.211
  144.7 2.3 copy.210
  147.0 2.2 copy.209
  155.9 2.2 copy.205
  160.4 2.4 copy.203
  165.0 2.2 copy.201
  179.9 5.4 collective-permute-start.7
  185.3 6.5 %collective-permute-start.6 = (bf16[1,64,8,32]{3,2,1,0:T(8,128)(2,1)}, bf16[1,64,8,32]{3,2,1,0:T(8,128)(2,1)}, u32[]{:S(2)}, u32[]{:S(2)}) collective-permute-start(bf16[1,64,8,32]{3,2,1,0:T(8,128)(2,1)} %bitcast.882), channel_id=1, source_target_pairs={{0,8},{8,16},{16,24},{24,32},{32,40},{40,48},{48,56},{56,64},{64,7... | collective-permute-start | bytes 98312 | tf_op jit(solution)/shard_map/ppermute | solution.py:13
  223.5 2.4 copy.185
  229.8 65.5 %reduce-scatter.2.cloned.1.call-done = f32[2,64,8,16]{1,2,0,3:T(8,128)} async-done(((f32[2,64,8,128]{1,2,0,3:T(8,128)}), f32[2,64,8,16]{1,2,0,3:T(8,128)}) %reduce-scatter.2.cloned.1.call-update) | async-done | bytes 65552 | tf_op jit(solution)/shard_map/reduce_scatter | solution.py:102
  297.3 4.4 all-to-all-start.1
  302.9 5.5 all-to-all-done.1
  335.2 86.9 %all-reduce.8.cloned.1.call-done = f32[27,128,32]{1,2,0:T(8,128)} async-done(((f32[27,128,32]{1,2,0:T(8,128)}), f32[27,128,32]{1,2,0:T(8,128)}) %all-reduce.8.cloned.1.call-update) | async-done | bytes 442384 | tf_op jit(solution)/shard_map/psum | solution.py:90
  423.9 152.3 %all-reduce.6.cloned.1.call-done = f32[27,128,128]{2,1,0:T(8,128)} async-done(((f32[27,128,128]{2,1,0:T(8,128)}), f32[27,128,128]{2,1,0:T(8,128)}) %all-reduce.6.cloned.1.call-update) | async-done | bytes 1769488 | tf_op jit(solution)/shard_map/psum | solution.py:117
  576.2 2.9 broadcast_multiply_fusion
  (366 shorter events, 123.2 us)
Async XLA Ops:
  8.0 287.2 %reduce-scatter.2.cloned.1.call-start = ((), (), s32[]{:S(2)}) async-start(), calls=%async_computation.3 | async-start | bytes 1179648 | tf_op jit(solution)/shard_map/reduce_scatter | solution.py:102
  8.9 6.4 %collective-permute-start = (bf16[1,16,16,128]{3,2,1,0:T(8,128)(2,1)S(1)}, bf16[1,16,16,128]{3,2,1,0:T(8,128)(2,1)S(1)}, u32[]{:S(2)}, u32[]{:S(2)}) collective-permute-start(bf16[1,16,16,128]{3,2,1,0:T(8,128)(2,1)S(1)} %get-tuple-element.112), channel_id=1, source_target_pairs={{0,8},{8,16},{16,24},{24,32},{32,40},{40,48},{48,56},{56,64},{64,7... | collective-permute-start | bytes 196616 | tf_op jit(solution)/shard_map/ppermute | solution.py:13
  13.4 5.6 collective-permute-start.1
  20.4 11.8 %copy-start.37 = (bf16[4,16,16,128]{3,2,1,0:T(8,128)(2,1)}, bf16[4,16,16,128]{3,2,1,0:T(8,128)(2,1)S(1)}, u32[]{:S(2)}) copy-start(bf16[4,16,16,128]{3,2,1,0:T(8,128)(2,1)S(1)} %get-tuple-element.110) | copy-start | bytes 786436
  20.4 15.7 %copy-start.31 = (bf16[4,16,16,128]{3,2,1,0:T(8,128)(2,1)}, bf16[4,16,16,128]{3,2,1,0:T(8,128)(2,1)S(1)}, u32[]{:S(2)}) copy-start(bf16[4,16,16,128]{3,2,1,0:T(8,128)(2,1)S(1)} %get-tuple-element.108) | copy-start | bytes 786436
  20.4 4.9 collective-permute-start.2
  24.0 4.8 collective-permute-start.3
  30.0 5.9 %copy-start.35 = (bf16[4,16,16,128]{3,2,1,0:T(8,128)(2,1)}, bf16[4,16,16,128]{3,2,1,0:T(8,128)(2,1)S(1)}, u32[]{:S(2)}) copy-start(bf16[4,16,16,128]{3,2,1,0:T(8,128)(2,1)S(1)} %get-tuple-element.77) | copy-start | bytes 786436
  30.0 6.4 %copy-start.33 = (bf16[4,16,16,128]{3,2,1,0:T(8,128)(2,1)}, bf16[4,16,16,128]{3,2,1,0:T(8,128)(2,1)S(1)}, u32[]{:S(2)}) copy-start(bf16[4,16,16,128]{3,2,1,0:T(8,128)(2,1)S(1)} %get-tuple-element.75) | copy-start | bytes 786436
  37.9 22.6 %copy-start.77 = (bf16[2,64,8,32]{1,3,2,0:T(8,128)(2,1)S(1)}, bf16[2,64,8,32]{1,3,2,0:T(8,128)(2,1)}, u32[]{:S(2)}) copy-start(bf16[2,64,8,32]{1,3,2,0:T(8,128)(2,1)} %param.7) | copy-start | bytes 196612
  54.5 7.5 %collective-permute-start.5 = (bf16[1,64,8,16]{3,2,1,0:T(8,128)(2,1)S(1)}, bf16[1,64,8,16]{3,2,1,0:T(8,128)(2,1)S(1)}, u32[]{:S(2)}, u32[]{:S(2)}) collective-permute-start(bf16[1,64,8,16]{3,2,1,0:T(8,128)(2,1)S(1)} %bitcast.885), channel_id=1, source_target_pairs={{8,0},{16,8},{24,16},{32,24},{40,32},{48,40},{56,48},{64,56},{72,6... | collective-permute-start | bytes 49160 | tf_op jit(solution)/shard_map/ppermute | solution.py:16
  56.8 5.6 collective-permute-start.4
  179.9 23.3 %copy-start.30 = (bf16[2,64,8,128]{3,2,1,0:T(8,128)(2,1)S(1)}, bf16[2,64,8,128]{3,2,1,0:T(8,128)(2,1)}, u32[]{:S(2)}) copy-start(bf16[2,64,8,128]{3,2,1,0:T(8,128)(2,1)} %copy.201) | copy-start | bytes 786436
  179.9 24.0 %copy-start.27 = (bf16[2,64,8,128]{3,2,1,0:T(8,128)(2,1)S(1)}, bf16[2,64,8,128]{3,2,1,0:T(8,128)(2,1)}, u32[]{:S(2)}) copy-start(bf16[2,64,8,128]{3,2,1,0:T(8,128)(2,1)} %copy.202) | copy-start | bytes 786436
  179.9 24.8 %copy-start.25 = (bf16[2,64,8,128]{3,2,1,0:T(8,128)(2,1)S(1)}, bf16[2,64,8,128]{3,2,1,0:T(8,128)(2,1)}, u32[]{:S(2)}) copy-start(bf16[2,64,8,128]{3,2,1,0:T(8,128)(2,1)} %copy.203) | copy-start | bytes 786436
  179.9 25.6 %copy-start.23 = (bf16[2,64,8,128]{3,2,1,0:T(8,128)(2,1)S(1)}, bf16[2,64,8,128]{3,2,1,0:T(8,128)(2,1)}, u32[]{:S(2)}) copy-start(bf16[2,64,8,128]{3,2,1,0:T(8,128)(2,1)} %copy.204) | copy-start | bytes 786436
  179.9 33.6 %collective-permute-start.7 = (bf16[1,64,8,32]{3,2,1,0:T(8,128)(2,1)}, bf16[1,64,8,32]{3,2,1,0:T(8,128)(2,1)}, u32[]{:S(2)}, u32[]{:S(2)}) collective-permute-start(bf16[1,64,8,32]{3,2,1,0:T(8,128)(2,1)} %bitcast.883), channel_id=1, source_target_pairs={{8,0},{16,8},{24,16},{32,24},{40,32},{48,40},{56,48},{64,56},{72,6... | collective-permute-start | bytes 98312 | tf_op jit(solution)/shard_map/ppermute | solution.py:16
  185.3 28.2 %collective-permute-start.6 = (bf16[1,64,8,32]{3,2,1,0:T(8,128)(2,1)}, bf16[1,64,8,32]{3,2,1,0:T(8,128)(2,1)}, u32[]{:S(2)}, u32[]{:S(2)}) collective-permute-start(bf16[1,64,8,32]{3,2,1,0:T(8,128)(2,1)} %bitcast.882), channel_id=1, source_target_pairs={{0,8},{8,16},{16,24},{24,32},{32,40},{40,48},{48,56},{56,64},{64,7... | collective-permute-start | bytes 98312 | tf_op jit(solution)/shard_map/ppermute | solution.py:13
  193.6 12.7 %copy-start.21 = (bf16[2,64,8,128]{3,2,1,0:T(8,128)(2,1)S(1)}, bf16[2,64,8,128]{3,2,1,0:T(8,128)(2,1)}, u32[]{:S(2)}) copy-start(bf16[2,64,8,128]{3,2,1,0:T(8,128)(2,1)} %copy.205) | copy-start | bytes 786436
  195.3 11.8 %copy-start.19 = (bf16[2,64,8,128]{3,2,1,0:T(8,128)(2,1)S(1)}, bf16[2,64,8,128]{3,2,1,0:T(8,128)(2,1)}, u32[]{:S(2)}) copy-start(bf16[2,64,8,128]{3,2,1,0:T(8,128)(2,1)} %copy.206) | copy-start | bytes 786436
  197.1 10.8 %copy-start.17 = (bf16[2,64,8,128]{3,2,1,0:T(8,128)(2,1)S(1)}, bf16[2,64,8,128]{3,2,1,0:T(8,128)(2,1)}, u32[]{:S(2)}) copy-start(bf16[2,64,8,128]{3,2,1,0:T(8,128)(2,1)} %copy.207) | copy-start | bytes 786436
  198.9 9.8 %copy-start.15 = (bf16[2,64,8,128]{3,2,1,0:T(8,128)(2,1)S(1)}, bf16[2,64,8,128]{3,2,1,0:T(8,128)(2,1)}, u32[]{:S(2)}) copy-start(bf16[2,64,8,128]{3,2,1,0:T(8,128)(2,1)} %copy.208) | copy-start | bytes 786436
  200.6 8.8 %copy-start.12 = (bf16[2,64,8,128]{3,2,1,0:T(8,128)(2,1)S(1)}, bf16[2,64,8,128]{3,2,1,0:T(8,128)(2,1)}, u32[]{:S(2)}) copy-start(bf16[2,64,8,128]{3,2,1,0:T(8,128)(2,1)} %copy.209) | copy-start | bytes 786436
  202.4 7.8 %copy-start.9 = (bf16[2,64,8,128]{3,2,1,0:T(8,128)(2,1)S(1)}, bf16[2,64,8,128]{3,2,1,0:T(8,128)(2,1)}, u32[]{:S(2)}) copy-start(bf16[2,64,8,128]{3,2,1,0:T(8,128)(2,1)} %copy.210) | copy-start | bytes 786436
  203.2 7.8 %copy-start.6 = (bf16[2,64,8,128]{3,2,1,0:T(8,128)(2,1)S(1)}, bf16[2,64,8,128]{3,2,1,0:T(8,128)(2,1)}, u32[]{:S(2)}) copy-start(bf16[2,64,8,128]{3,2,1,0:T(8,128)(2,1)} %copy.211) | copy-start | bytes 786436
  204.0 7.8 %copy-start.4 = (bf16[2,64,8,128]{3,2,1,0:T(8,128)(2,1)S(1)}, bf16[2,64,8,128]{3,2,1,0:T(8,128)(2,1)}, u32[]{:S(2)}) copy-start(bf16[2,64,8,128]{3,2,1,0:T(8,128)(2,1)} %copy.212) | copy-start | bytes 786436
  204.7 7.8 %copy-start.2 = (bf16[2,64,8,128]{3,2,1,0:T(8,128)(2,1)S(1)}, bf16[2,64,8,128]{3,2,1,0:T(8,128)(2,1)}, u32[]{:S(2)}) copy-start(bf16[2,64,8,128]{3,2,1,0:T(8,128)(2,1)} %copy.213) | copy-start | bytes 786436
  225.9 75.9 %copy-start.72 = (bf16[2,64,8,128]{3,2,1,0:T(8,128)(2,1)S(1)}, bf16[2,64,8,128]{3,2,1,0:T(8,128)(2,1)}, u32[]{:S(2)}) copy-start(bf16[2,64,8,128]{3,2,1,0:T(8,128)(2,1)} %copy.219) | copy-start | bytes 786436
  297.3 11.0 %all-to-all-start.1 = ((bf16[8,2,1024]{2,1,0:T(2,128)(2,1)}), bf16[8,2,1024]{2,1,0:T(2,128)(2,1)S(1)}, u32[]{:S(2)}, u32[]{:S(2)}) async-start(bf16[8,2,1024]{2,1,0:T(2,128)(2,1)} %reshape.422), calls=%async_computation.2 | async-start | bytes 65536 | tf_op jit(solution)/shard_map/all_to_all | solution.py:103
  301.8 120.3 %all-reduce.8.cloned.1.call-start = ((), (), s32[]{:S(2)}) async-start(), calls=%async_computation.5 | async-start | bytes 884736 | tf_op jit(solution)/shard_map/psum | solution.py:90
  302.6 6.8 %copy-start.76 = (f32[1024,128]{1,0:T(8,128)S(1)}, f32[1024,128]{1,0:T(8,128)}, u32[]{:S(2)}) copy-start(f32[1024,128]{1,0:T(8,128)} %get-tuple-element.118) | copy-start | bytes 1572868
  302.6 273.5 %all-reduce.6.cloned.1.call-start = ((), (), s32[]{:S(2)}) async-start(), calls=%async_computation.4 | async-start | bytes 3538944 | tf_op jit(solution)/shard_map/psum | solution.py:117
  (60 other events, 206.9 us)
Sparse Core Ops, SparseCore 0:
  226.0 69.1 reduce-scatter.1
Sparse Core Ops, SparseCore 1:
  305.3 116.7 all-reduce.7
  427.3 148.8 all-reduce.5
where the time goes:
time: 595 us; the launch traced here: 587 us
  waiting for transfers between devices  318 us (53%)
  local copies, waits for them, and re-layouts  87 us (15%)
  matrix products  73.5 us (12%)
  blocking collectives  46.9 us (8%)
  starting transfers between devices  33.9 us (6%)
  between operations  17.3 us (3%)
  other arithmetic  10.6 us (2%)
    psum x1, waiting for transfers between devices, shards(): lax.psum(early_terms, ('space', 'filt')) / math.sqrt(early_total)  152 us
    psum x1, waiting for transfers between devices, shards(): grad_deep = lax.psum(deep_terms, 'space') / math.sqrt(deep_total)  86.9 us
    reduce_scatter x1, waiting for transfers between devices, shards(): lax.psum_scatter(term, 'filt', scatter_dimension=3, tiled=True)  65.5 us
    unnamed x194, local copies, waits for them, and re-layouts  59.2 us
    dot_general x54, matrix products, contract_cells(): lax.dot_general(left, right, (((0,), (0,)), ((), ())), preferred_element_...  51.3 us
    all_gather x1, blocking collectives, shards(): piece = lax.all_gather(slab, 'filt', axis=3, tiled=True)  32.5 us
    slice x5, local copies, waits for them, and re-layouts, window(): source[first:first + size_x, second:second + size_y, third:third + size_z]  19 us
    ppermute x4, starting transfers between devices, extended(): lax.ppermute(lax.slice_in_dim(block, block.shape[dim] - width, None, axis...  18.3 us
  transfers between devices with their start and end apart: 12, of which 7 were waited for; matrix products, arithmetic and copies ran while one was open for 10% of the time, Pallas kernels for 0%

commit v1 on v0

--- a/solution.py
+++ b/solution.py
@@ -73,7 +73,9 @@
 
     empty = jnp.zeros((deep_cells, filters), jnp.float32)
     total = empty
-    piece = lax.all_gather(slab, "filt", axis=3, tiled=True)
+    piece = jnp.concatenate(
+        lax.all_to_all(jnp.stack([slab] * lax.axis_size("filt")), "filt", 0, 0), axis=3
+    )
     for forward_tap in range(27):
         rows = w_deep[forward_tap]
         total = total + jnp.dot(

time: 595 us -> 684 us (1.15)
  local copies, waits for them, and re-layouts: 87 us -> 156 us
  blocking collectives: 46.9 us -> 63.3 us
  waiting for transfers between devices: 318 us -> 311 us
    slice x5 -> x34, local copies, waits for them, and re-layouts: 19 us -> 77 us  [window(): source[first:first + size_x, second:second + size_y, third:third + size_z]]
    all_gather x1, blocking collectives: 32.5 us -> 45.5 us  [shards(): deep_terms = kernel_terms(lax.all_gather(slab, 'filt', axis=3, tiled=True))]
    unnamed x194 -> x207, local copies, waits for them, and re-layouts: 59.2 us -> 66.1 us
  transfers between devices with their start and end apart: 12 -> 13, of which waited for: 7 -> 7; matrix products, arithmetic and copies ran while one was open for 10% -> 21% of each run, Pallas kernels for 0% -> 0%
where the time goes in v1:
time: 684 us; the launch traced here: 673 us
  waiting for transfers between devices  311 us (45%)
  local copies, waits for them, and re-layouts  156 us (23%)
  matrix products  73.6 us (11%)
  blocking collectives  63.3 us (9%)
  starting transfers between devices  38.9 us (6%)
  between operations  17.3 us (3%)
  other arithmetic  12.9 us (2%)
    psum x1, waiting for transfers between devices, shards(): lax.psum(early_terms, ('space', 'filt')) / math.sqrt(early_total)  152 us
    psum x1, waiting for transfers between devices, shards(): grad_deep = lax.psum(deep_terms, 'space') / math.sqrt(deep_total)  85.9 us
    slice x34, local copies, waits for them, and re-layouts, window(): source[first:first + size_x, second:second + size_y, third:third + size_z]  77 us
    unnamed x207, local copies, waits for them, and re-layouts  66.1 us
    reduce_scatter x1, waiting for transfers between devices, shards(): lax.psum_scatter(term, 'filt', scatter_dimension=3, tiled=True)  61.5 us
    dot_general x54, matrix products, contract_cells(): lax.dot_general(left, right, (((0,), (0,)), ((), ())), preferred_element_...  52.2 us
    all_gather x1, blocking collectives, shards(): deep_terms = kernel_terms(lax.all_gather(slab, 'filt', axis=3, tiled=True))  45.5 us
    ppermute x4, starting transfers between devices, extended(): lax.ppermute(lax.slice_in_dim(block, block.shape[dim] - width, None, axis...  21 us
  transfers between devices with their start and end apart: 13, of which 7 were waited for; matrix products, arithmetic and copies ran while one was open for 21% of the time, Pallas kernels for 0%

profile of v1, /device:TPU:1, one launch (start us, length us, event | category | flops | bytes accessed | tf_op | source)
XLA Modules:
  0.0 672.6 jit_solution(6179140995483306878)
XLA Ops:
  8.9 4.5 collective-permute-start
  15.4 3.6 collective-permute-done.1
  21.6 4.2 collective-permute-start.2
  36.9 17.8 %all_to_all.32 = bf16[8,2,1024]{2,1,0:T(2,128)(2,1)S(1)} all-to-all(bf16[8,2,1024]{2,1,0:T(2,128)(2,1)S(1)} %reshape.511), channel_id=1, replica_groups=mesh['space'=16,'filt'=8] {'filt'}, dimensions={0} | all-to-all | bytes 65536 | tf_op jit(solution)/shard_map/all_to_all | solution.py:59
  56.6 2.3 collective-permute-start.5
  59.6 4.4 collective-permute-start.4
  71.3 3.6 all-to-all-start.1
  74.9 45.5 %all_gather.3 = bf16[4,66,10,128]{1,0,2,3:T(4,128)(2,1)S(1)} all-gather(bf16[4,66,10,16]{1,0,2,3:T(4,128)(2,1)} %copy.306), channel_id=1, replica_groups=mesh['space'=16,'filt'=8] {'filt'}, dimensions={3}, use_global_device_ids=true | all-gather | bytes 760320 | tf_op jit(solution)/shard_map/all_gather | solution.py:90
  120.4 12.4 %fusion.254 = (bf16[2,64,8,128]{1,0,2,3:T(2,128)(2,1)}, bf16[2,64,8,128]{1,0,2,3:T(2,128)(2,1)}, bf16[2,64,8,128]{1,0,2,3:T(2,128)(2,1)}, bf16[2,64,8,128]{1,0,2...) fusion(bf16[4,66,10,128]{1,0,2,3:T(4,128)(2,1)S(1)} %all_gather.3), kind=kLoop, calls=%fused_computation.421 | loop fusion | bytes 9961472 | tf_op jit(solution)/shard_map/slice | solution.py:30
  132.8 5.0 fusion.255
  144.5 2.3 copy.341
  146.8 2.3 copy.342
  155.8 2.3 copy.346
  160.3 2.3 copy.348
  164.8 2.3 copy.350
  169.3 2.3 copy.352
  180.5 2.3 copy.357
  182.8 2.3 copy.358
  185.1 2.3 copy.359
  189.6 2.3 copy.361
  191.8 2.3 copy.362
  194.1 2.4 copy.363
  199.1 2.8 fusion.257
  201.9 4.5 fusion.256
  268.2 4.1 collective-permute-start.7
  273.1 7.9 %collective-permute-start.6 = (bf16[1,64,8,32]{3,2,1,0:T(8,128)(2,1)}, bf16[1,64,8,32]{3,2,1,0:T(8,128)(2,1)}, u32[]{:S(2)}, u32[]{:S(2)}) collective-permute-start(bf16[1,64,8,32]{3,2,1,0:T(8,128)(2,1)} %bitcast.915), channel_id=1, source_target_pairs={{0,8},{8,16},{16,24},{24,32},{32,40},{40,48},{48,56},{56,64},{64,7... | collective-permute-start | bytes 98312 | tf_op jit(solution)/shard_map/ppermute | solution.py:13
  319.5 61.5 %reduce-scatter.2.cloned.1.call-done = f32[2,64,8,16]{1,2,0,3:T(8,128)} async-done(((f32[2,64,8,128]{1,2,0,3:T(8,128)}), f32[2,64,8,16]{1,2,0,3:T(8,128)}) %reduce-scatter.2.cloned.1.call-update) | async-done | bytes 65552 | tf_op jit(solution)/shard_map/reduce_scatter | solution.py:104
  383.1 4.4 all-to-all-start.2
  388.7 5.5 all-to-all-done.2
  422.1 85.9 %all-reduce.8.cloned.1.call-done = f32[27,128,32]{1,2,0:T(8,128)} async-done(((f32[27,128,32]{1,2,0:T(8,128)}), f32[27,128,32]{1,2,0:T(8,128)}) %all-reduce.8.cloned.1.call-update) | async-done | bytes 442384 | tf_op jit(solution)/shard_map/psum | solution.py:92
  509.8 152.3 %all-reduce.6.cloned.1.call-done = f32[27,128,128]{2,1,0:T(8,128)} async-done(((f32[27,128,128]{2,1,0:T(8,128)}), f32[27,128,128]{2,1,0:T(8,128)}) %all-reduce.6.cloned.1.call-update) | async-done | bytes 1769488 | tf_op jit(solution)/shard_map/psum | solution.py:119
  662.0 2.9 broadcast_multiply_fusion
  (413 shorter events, 192.8 us)
Async XLA Ops:
  8.9 6.4 collective-permute-start
  13.4 5.6 collective-permute-start.1
  20.3 9.9 %copy-start.5 = (bf16[4,16,16,128]{3,2,1,0:T(8,128)(2,1)}, bf16[4,16,16,128]{3,2,1,0:T(8,128)(2,1)S(1)}, u32[]{:S(2)}) copy-start(bf16[4,16,16,128]{3,2,1,0:T(8,128)(2,1)S(1)} %get-tuple-element.137) | copy-start | bytes 786436
  20.3 5.5 collective-permute-start.3
  21.6 5.1 collective-permute-start.2
  35.9 28.1 %copy-start.84 = (bf16[2,64,8,32]{1,3,2,0:T(8,128)(2,1)S(1)}, bf16[2,64,8,32]{1,3,2,0:T(8,128)(2,1)}, u32[]{:S(2)}) copy-start(bf16[2,64,8,32]{1,3,2,0:T(8,128)(2,1)} %param.7) | copy-start | bytes 196612
  56.6 8.9 %collective-permute-start.5 = (bf16[1,64,8,16]{3,2,1,0:T(8,128)(2,1)}, bf16[1,64,8,16]{3,2,1,0:T(8,128)(2,1)}, u32[]{:S(2)}, u32[]{:S(2)}) collective-permute-start(bf16[1,64,8,16]{3,2,1,0:T(8,128)(2,1)} %bitcast.60), channel_id=1, source_target_pairs={{8,0},{16,8},{24,16},{32,24},{40,32},{48,40},{56,48},{64,56},{72,6... | collective-permute-start | bytes 49160 | tf_op jit(solution)/shard_map/ppermute | solution.py:16
  59.6 6.6 collective-permute-start.4
  71.3 127.5 %all-to-all-start.1 = ((bf16[8,4,66,10,16]{2,4,3,1,0:T(8,128)(2,1)}), bf16[8,4,66,10,16]{2,4,3,1,0:T(8,128)(2,1)S(1)}, u32[]{:S(2)}, u32[]{:S(2)}) async-start(bf16[8,4,66,10,16]{2,4,3,1,0:T(8,128)(2,1)} %stack.179), calls=%async_computation.1 | async-start | bytes 2621440 | tf_op jit(solution)/shard_map/all_to_all | solution.py:77
  74.8 306.2 %reduce-scatter.2.cloned.1.call-start = ((), (), s32[]{:S(2)}) async-start(), calls=%async_computation.4 | async-start | bytes 1179648 | tf_op jit(solution)/shard_map/reduce_scatter | solution.py:104
  266.3 23.5 %copy-start.58 = (bf16[2,64,8,128]{3,2,1,0:T(8,128)(2,1)S(1)}, bf16[2,64,8,128]{3,2,1,0:T(8,128)(2,1)}, u32[]{:S(2)}) copy-start(bf16[2,64,8,128]{3,2,1,0:T(8,128)(2,1)} %copy.343) | copy-start | bytes 786436
  266.5 24.1 %copy-start.56 = (bf16[2,64,8,128]{3,2,1,0:T(8,128)(2,1)S(1)}, bf16[2,64,8,128]{3,2,1,0:T(8,128)(2,1)}, u32[]{:S(2)}) copy-start(bf16[2,64,8,128]{3,2,1,0:T(8,128)(2,1)} %copy.344) | copy-start | bytes 786436
  266.6 24.8 %copy-start.57 = (bf16[2,64,8,128]{3,2,1,0:T(8,128)(2,1)S(1)}, bf16[2,64,8,128]{3,2,1,0:T(8,128)(2,1)}, u32[]{:S(2)}) copy-start(bf16[2,64,8,128]{3,2,1,0:T(8,128)(2,1)} %copy.345) | copy-start | bytes 786436
  267.4 24.7 %copy-start.55 = (bf16[2,64,8,128]{3,2,1,0:T(8,128)(2,1)S(1)}, bf16[2,64,8,128]{3,2,1,0:T(8,128)(2,1)}, u32[]{:S(2)}) copy-start(bf16[2,64,8,128]{3,2,1,0:T(8,128)(2,1)} %copy.346) | copy-start | bytes 786436
  267.4 25.5 %copy-start.54 = (bf16[2,64,8,128]{3,2,1,0:T(8,128)(2,1)S(1)}, bf16[2,64,8,128]{3,2,1,0:T(8,128)(2,1)}, u32[]{:S(2)}) copy-start(bf16[2,64,8,128]{3,2,1,0:T(8,128)(2,1)} %copy.347) | copy-start | bytes 786436
  268.2 34.2 %collective-permute-start.7 = (bf16[1,64,8,32]{3,2,1,0:T(8,128)(2,1)}, bf16[1,64,8,32]{3,2,1,0:T(8,128)(2,1)}, u32[]{:S(2)}, u32[]{:S(2)}) collective-permute-start(bf16[1,64,8,32]{3,2,1,0:T(8,128)(2,1)} %bitcast.914), channel_id=1, source_target_pairs={{8,0},{16,8},{24,16},{32,24},{40,32},{48,40},{56,48},{64,56},{72,6... | collective-permute-start | bytes 98312 | tf_op jit(solution)/shard_map/ppermute | solution.py:16
  273.1 20.6 %copy-start.53 = (bf16[2,64,8,128]{3,2,1,0:T(8,128)(2,1)S(1)}, bf16[2,64,8,128]{3,2,1,0:T(8,128)(2,1)}, u32[]{:S(2)}) copy-start(bf16[2,64,8,128]{3,2,1,0:T(8,128)(2,1)} %copy.348) | copy-start | bytes 786436
  273.1 29.4 %collective-permute-start.6 = (bf16[1,64,8,32]{3,2,1,0:T(8,128)(2,1)}, bf16[1,64,8,32]{3,2,1,0:T(8,128)(2,1)}, u32[]{:S(2)}, u32[]{:S(2)}) collective-permute-start(bf16[1,64,8,32]{3,2,1,0:T(8,128)(2,1)} %bitcast.915), channel_id=1, source_target_pairs={{0,8},{8,16},{16,24},{24,32},{32,40},{40,48},{48,56},{56,64},{64,7... | collective-permute-start | bytes 98312 | tf_op jit(solution)/shard_map/ppermute | solution.py:13
  282.7 11.7 %copy-start.52 = (bf16[2,64,8,128]{3,2,1,0:T(8,128)(2,1)S(1)}, bf16[2,64,8,128]{3,2,1,0:T(8,128)(2,1)}, u32[]{:S(2)}) copy-start(bf16[2,64,8,128]{3,2,1,0:T(8,128)(2,1)} %copy.349) | copy-start | bytes 786436
  284.5 10.8 %copy-start.51 = (bf16[2,64,8,128]{3,2,1,0:T(8,128)(2,1)S(1)}, bf16[2,64,8,128]{3,2,1,0:T(8,128)(2,1)}, u32[]{:S(2)}) copy-start(bf16[2,64,8,128]{3,2,1,0:T(8,128)(2,1)} %copy.350) | copy-start | bytes 786436
  286.3 9.8 %copy-start.50 = (bf16[2,64,8,128]{3,2,1,0:T(8,128)(2,1)S(1)}, bf16[2,64,8,128]{3,2,1,0:T(8,128)(2,1)}, u32[]{:S(2)}) copy-start(bf16[2,64,8,128]{3,2,1,0:T(8,128)(2,1)} %copy.351) | copy-start | bytes 786436
  288.0 8.8 %copy-start.49 = (bf16[2,64,8,128]{3,2,1,0:T(8,128)(2,1)S(1)}, bf16[2,64,8,128]{3,2,1,0:T(8,128)(2,1)}, u32[]{:S(2)}) copy-start(bf16[2,64,8,128]{3,2,1,0:T(8,128)(2,1)} %copy.352) | copy-start | bytes 786436
  289.8 7.8 %copy-start.48 = (bf16[2,64,8,128]{3,2,1,0:T(8,128)(2,1)S(1)}, bf16[2,64,8,128]{3,2,1,0:T(8,128)(2,1)}, u32[]{:S(2)}) copy-start(bf16[2,64,8,128]{3,2,1,0:T(8,128)(2,1)} %copy.353) | copy-start | bytes 786436
  290.6 7.8 %copy-start.47 = (bf16[2,64,8,128]{3,2,1,0:T(8,128)(2,1)S(1)}, bf16[2,64,8,128]{3,2,1,0:T(8,128)(2,1)}, u32[]{:S(2)}) copy-start(bf16[2,64,8,128]{3,2,1,0:T(8,128)(2,1)} %copy.354) | copy-start | bytes 786436
  291.4 7.8 %copy-start.46 = (bf16[2,64,8,128]{3,2,1,0:T(8,128)(2,1)S(1)}, bf16[2,64,8,128]{3,2,1,0:T(8,128)(2,1)}, u32[]{:S(2)}) copy-start(bf16[2,64,8,128]{3,2,1,0:T(8,128)(2,1)} %copy.355) | copy-start | bytes 786436
  292.1 7.8 %copy-start.45 = (bf16[2,64,8,128]{3,2,1,0:T(8,128)(2,1)S(1)}, bf16[2,64,8,128]{3,2,1,0:T(8,128)(2,1)}, u32[]{:S(2)}) copy-start(bf16[2,64,8,128]{3,2,1,0:T(8,128)(2,1)} %copy.356) | copy-start | bytes 786436
  292.9 7.8 %copy-start.44 = (bf16[2,64,8,128]{3,2,1,0:T(8,128)(2,1)S(1)}, bf16[2,64,8,128]{3,2,1,0:T(8,128)(2,1)}, u32[]{:S(2)}) copy-start(bf16[2,64,8,128]{3,2,1,0:T(8,128)(2,1)} %copy.357) | copy-start | bytes 786436
  293.7 7.8 %copy-start.43 = (bf16[2,64,8,128]{3,2,1,0:T(8,128)(2,1)S(1)}, bf16[2,64,8,128]{3,2,1,0:T(8,128)(2,1)}, u32[]{:S(2)}) copy-start(bf16[2,64,8,128]{3,2,1,0:T(8,128)(2,1)} %copy.358) | copy-start | bytes 786436
  313.7 73.9 %copy-start.39 = (bf16[2,64,8,128]{3,2,1,0:T(8,128)(2,1)S(1)}, bf16[2,64,8,128]{3,2,1,0:T(8,128)(2,1)}, u32[]{:S(2)}) copy-start(bf16[2,64,8,128]{3,2,1,0:T(8,128)(2,1)} %copy.364) | copy-start | bytes 786436
  383.1 11.0 %all-to-all-start.2 = ((bf16[8,2,1024]{2,1,0:T(2,128)(2,1)}), bf16[8,2,1024]{2,1,0:T(2,128)(2,1)S(1)}, u32[]{:S(2)}, u32[]{:S(2)}) async-start(bf16[8,2,1024]{2,1,0:T(2,128)(2,1)} %reshape.513), calls=%async_computation.3 | async-start | bytes 65536 | tf_op jit(solution)/shard_map/all_to_all | solution.py:105
  387.6 120.4 %all-reduce.8.cloned.1.call-start = ((), (), s32[]{:S(2)}) async-start(), calls=%async_computation.6 | async-start | bytes 884736 | tf_op jit(solution)/shard_map/psum | solution.py:92
  388.4 273.6 %all-reduce.6.cloned.1.call-start = ((), (), s32[]{:S(2)}) async-start(), calls=%async_computation.5 | async-start | bytes 3538944 | tf_op jit(solution)/shard_map/psum | solution.py:119
  (68 other events, 247.4 us)
Sparse Core Ops, SparseCore 0:
  313.8 67.1 reduce-scatter.1
Sparse Core Ops, SparseCore 1:
  391.1 116.8 all-reduce.7
  513.2 148.8 all-reduce.5
